TPU v7x, 32 devices: a whole 2x2x4 slice. The times are simulated.
32 devices in a mesh: section: 4 (over y, x), vocab: 8 (over z, core), dp: 1.
Axes of the slice: x: 2, y: 2, z: 4, core: 2. Of those that a mesh axis runs over, the one named last changes fastest.
Arguments:
- hidden: bfloat16 [1, 512, 3072], P('dp', ('section', 'vocab')), may hold values from -160 to 160
- head: bfloat16 [131072, 3072], P(('section', 'vocab')), may hold values from -3 to 3
- labels: int32 [1, 512], P('dp'), may hold values from 0 to 131071
- response_mask: int32 [1, 512], P('dp'), may hold values from 0 to 1, as said below
- seq_pair: int32 [1, 4], P('dp'), may hold values from 0 to 3, as said below
- ref_logp: float32 [4], replicated, may hold values from -12.6 to -12.4
Outputs:
- token_logprob: float32 [1, 512], P('dp', ('section', 'vocab'))
- pair_margin: float32 [2], replicated
- loss: float32 [], replicated
Inputs may be any that keep to these rules, and one draw needn't show every extreme that they name: `response_mask`: each sequence of 128 rows has more than half of its rows set. `seq_pair`: over all replicas every slot of 0 to 3 appears once; slot q belongs to pair q // 2 and is its chosen response when q is even.
All inputs are finite; a program needn't handle non-finite values.
Results may differ from a plain program's by a relative error of at most 0.0003.
Values may be sent and summed in bfloat16 or wider, within the bound.
A program may use at most 64 MiB of HBM per device.

v0:
```python
import jax
import jax.numpy as jnp
from jax import lax
from jax.sharding import PartitionSpec as P

SEQ_DP = 4


beta_scale = 5.0


def body(hidden, head, labels, response_mask, seq_pair, ref_logp):
    shard_rows = hidden.shape[1]
    vocab_rows = head.shape[0]
    chip_rows = lax.all_gather(hidden, "vocab", axis=1, tiled=True)
    gathered = lax.all_gather(chip_rows, "section", axis=1, tiled=True)
    logits = lax.dot_general(
        gathered[0], head, (((1,), (1,)), ((), ())), preferred_element_type=jnp.float32
    )
    position = lax.axis_index(("section", "vocab"))
    local_max = jnp.max(logits, axis=1)
    local_sum = jnp.sum(jnp.exp(logits - local_max[:, None]), axis=1)
    target = labels[0] - position * vocab_rows
    column = lax.broadcasted_iota(jnp.int32, logits.shape, 1)
    label_part = jnp.sum(jnp.where(column == target[:, None], logits, 0.0), axis=1)
    whole_max = lax.pmax(local_max, ("section", "vocab"))
    total, label_logit = lax.psum(
        (local_sum * jnp.exp(local_max - whole_max), label_part), ("section", "vocab")
    )
    logprob = label_logit - whole_max - jnp.log(total)
    own_rows = lax.dynamic_slice_in_dim(logprob, position * shard_rows, shard_rows)
    token_logprob = own_rows[None, :]
    all_rows = logprob.shape[0]
    seq_len = all_rows // SEQ_DP
    slot_count = ref_logp.shape[0]
    weights = response_mask[0].astype(jnp.float32)
    counts = jnp.sum(weights.reshape(SEQ_DP, seq_len), axis=1)
    slot_ids = lax.broadcasted_iota(jnp.int32, (SEQ_DP, slot_count), 1)
    in_pair = (seq_pair[0][:, None] == slot_ids).astype(jnp.float32)
    seq_sums = jnp.sum((logprob * weights).reshape(SEQ_DP, seq_len), axis=1)
    seq_means = seq_sums / counts
    policy = lax.psum(jnp.sum(in_pair * seq_means[:, None], axis=0), "dp")
    pair_margin = beta_scale * (policy[0::2] - ref_logp[0::2] - (policy[1::2] - ref_logp[1::2]))
    loss = jnp.mean(jnp.logaddexp(0.0, -pair_margin))
    return (token_logprob, pair_margin, loss)


def solution(mesh):
    placed = (
        P("dp", ("section", "vocab"), None),
        P(("section", "vocab"), None),
        P("dp", None),
        P("dp", None),
        P("dp", None),
        P(),
    )
    return jax.shard_map(
        body,
        mesh=mesh,
        in_specs=placed,
        out_specs=(P("dp", ("section", "vocab")), P(), P()),
        check_vma=False,
    )
```

profile of v0, /device:TPU:0, one launch (start us, length us, event | category | flops | bytes accessed | tf_op | source)
XLA Modules:
  0.0 187.5 jit_solution(17460948723642342068)
XLA Ops:
  7.2 0.0 all-gather.2.cloned.1.call-start
  7.2 18.5 %all_gather.6 = bf16[1,128,3072]{2,1,0:T(8,128)(2,1)} all-gather(bf16[1,16,3072]{2,1,0:T(8,128)(2,1)} %param.6), channel_id=1, replica_groups=mesh['section'=4,'vocab'=8,'dp'=1] {'vocab'}, dimensions={1}, use_global_device_ids=true | all-gather | bytes 884736 | tf_op jit(solution)/shard_map/all_gather | solution.py:15
  25.7 0.0 all-gather.2.cloned.1.call-update
  25.8 0.7 slice.13
  26.5 0.7 slice.15
  27.2 0.7 convert_element_type.15
  27.9 0.1 reduce_sum.57
  28.0 0.7 broadcast_subtract_fusion
  28.7 41.9 %all-gather.2.cloned.1.call-done = bf16[1,512,3072]{2,1,0:T(8,128)(2,1)} async-done(((bf16[1,128,3072]{2,1,0:T(8,128)(2,1)}), bf16[1,512,3072]{2,1,0:T(8,128)(2,1)}) %all-gather.2.cloned.1.call-update) | async-done | bytes 3145744 | tf_op jit(solution)/shard_map/all_gather | solution.py:16
  70.6 21.0 %fusion.3 = (f32[512]{0:T(512)S(1)}, f32[512,4096]{1,0:T(8,128)}) fusion(bf16[4096,3072]{1,0:T(8,128)(2,1)} %param.7, bf16[1,512,3072]{2,1,0:T(8,128)(2,1)} %all-gather.2.cloned.1.call-done), kind=kOutput, calls=%fused_computation.15 | convolution fusion | flops 12886999040 | bytes 36702208 | tf_op jit(solution)/shard_map/dot_general | solution.py:17
  91.6 0.0 copy-start
  91.6 39.2 %pmax.7 = f32[512]{0:T(512)S(1)} all-reduce(f32[512]{0:T(512)S(1)} %get-tuple-element.11), channel_id=1, replica_groups=mesh['section'=4,'vocab'=8,'dp'=1] {'section','vocab'}, use_global_device_ids=true, to_apply=%region_3.4 | all-reduce | flops 512 | bytes 4096 | tf_op jit(solution)/shard_map/pmax | solution.py:26
  130.9 4.9 %select_reduce_fusion = (f32[512]{0:T(512)S(1)}, f32[512]{0:T(512)S(1)}) fusion(f32[512,4096]{1,0:T(8,128)} %get-tuple-element.12, s32[512]{0:T(512)S(1)} %bitcast.16, f32[512]{0:T(512)S(1)} %get-tuple-element.11), kind=kLoop, calls=%fused_computation.1 | loop fusion | flops 10484736 | bytes 8396800 | tf_op jit(solution)/shard_map/reduce_sum | solution.py:25
  135.8 40.9 %all-reduce = (f32[512]{0:T(512)S(1)}, f32[512]{0:T(512)S(1)}) all-reduce(f32[512]{0:T(512)S(1)} %exponential_multiply_fusion, f32[512]{0:T(512)S(1)} %get-tuple-element.3), channel_id=1, replica_groups=mesh['section'=4,'vocab'=8,'dp'=1] {'section','vocab'}, use_global_device_ids=true, to_apply=%region_5.6 | all-reduce | flops 1024 | bytes 8192 | tf_op jit(solution)/shard_map/psum | solution.py:27
  176.8 0.1 bitcast_reduce_fusion
  176.9 0.0 copy-done
  176.9 0.1 select_reduce_fusion.1
  177.0 0.1 slice.12
  177.1 0.1 slice.14
  177.2 1.1 fusion.2
  178.9 0.6 dynamic-slice_bitcast_fusion
  (2 shorter events, 0.0 us)
Async XLA Ops:
  7.2 63.5 %all-gather.2.cloned.1.call-start = ((), (), s32[]{:S(2)}) async-start(), calls=%async_computation | async-start | bytes 3932160 | tf_op jit(solution)/shard_map/all_gather | solution.py:16
  91.6 85.3 %copy-start = (s32[1,4]{1,0:T(1,128)S(1)}, s32[1,4]{1,0:T(1,128)}, u32[]{:S(2)}) copy-start(s32[1,4]{1,0:T(1,128)} %param.10) | copy-start | bytes 52
Sparse Core Ops, SparseCore 0:
  25.9 44.7 all-gather.1
where the time goes:
time: 188 us
  blocking collectives  98.7 us (52%)
  waiting for transfers between devices  41.9 us (22%)
  matrix products  21 us (11%)
  between operations  15.8 us (8%)
  other arithmetic  7.75 us (4%)
  local copies, waits for them, and re-layouts  2.27 us (1%)
    all_gather x1, waiting for transfers between devices, body(): gathered = lax.all_gather(chip_rows, 'section', axis=1, tiled=True)  41.9 us
    psum x1, blocking collectives, body(): lax.psum((local_sum * jnp.exp(local_max - whole_max), label_part), ('sect...  40.9 us
    pmax x1, blocking collectives, body(): whole_max = lax.pmax(local_max, ('section', 'vocab'))  39.2 us
    dot_general x1, matrix products, body(): lax.dot_general(gathered[0], head, (((1,), (1,)), ((), ())), preferred_el...  21 us
    all_gather x1, blocking collectives, body(): chip_rows = lax.all_gather(hidden, 'vocab', axis=1, tiled=True)  18.5 us
    reduce_sum x1, other arithmetic, body(): jnp.sum(jnp.where(column == target[:, None], logits, 0.0), axis=1)  4.93 us
  transfers between devices with their start and end apart: 1, of which 1 were waited for; matrix products, arithmetic and copies ran while one was open for 2% of the time, Pallas kernels for 0%

commit v1 on v0

v1 whole, which is shorter than its diff:
```python
import functools

import jax
import jax.numpy as jnp
from jax import lax
from jax.experimental import pallas as pl
from jax.experimental.pallas import tpu as pltpu
from jax.sharding import PartitionSpec as P

SEQ_DP = 4
CORES = 2
LANES = 128
CHUNKS = 4
TILE = 512
SEGMENTS = 4
LOWEST = -3.0e38

beta_scale = 5.0
MESH = pl.DeviceIdType.MESH


def kernel(
    sections,
    vocab,
    solo,
    hidden_ref,
    head_ref,
    labels_ref,
    mask_ref,
    pair_ref,
    ref_ref,
    token_ref,
    policy_ref,
    margin_ref,
    loss_ref,
    hid,
    headv,
    acc,
    run_max,
    run_sum,
    run_label,
    target_ref,
    stat_a,
    stat_b,
    lp_ref,
    send_sem,
    recv_sem,
    own_sem,
    head_sem,
    stat_send,
    recv_a,
    recv_b,
):
    rows = hidden_ref.shape[1]
    vocab_rows, width = head_ref.shape
    chunk = width // CHUNKS
    all_rows = hid.shape[1]
    floors = vocab // CORES
    s = lax.axis_index("section")
    v = lax.axis_index("vocab")
    z, c = v // CORES, v % CORES
    position = s * vocab + v
    near_a = s + 1 - 2 * (s % 2)
    near_b = (s + 2) % 4
    n1 = (1 - c) * near_a + c * near_b
    n2 = c * near_a + (1 - c) * near_b
    far = 3 - s

    def head_copy(k):
        return pltpu.make_async_copy(
            head_ref.at[:, pl.ds(k * chunk, chunk)], headv.at[k], head_sem.at[k]
        )

    def own_copy(k):
        return pltpu.make_async_copy(
            hidden_ref.at[0, :, pl.ds(k * chunk, chunk)],
            hid.at[k, pl.ds(position * rows, rows)],
            own_sem.at[k],
        )

    def move(k, owner, to_s, to_v, own=False):
        here = hid.at[k, pl.ds(owner * rows, rows)]
        src = hidden_ref.at[0, :, pl.ds(k * chunk, chunk)] if own else here
        return pltpu.make_async_remote_copy(
            src_ref=src,
            dst_ref=here,
            send_sem=send_sem.at[k],
            recv_sem=recv_sem.at[k, owner],
            device_id={"section": to_s, "vocab": to_v},
            device_id_type=MESH,
        )

    other = z * CORES + 1 - c

    def arrived(k, owner):
        move(k, owner, s, other).wait_recv()

    def floor(dz):
        return ((z + dz) % floors) * CORES

    def stage0(k):
        own_copy(k).start()
        for dz in range(1, floors):
            move(k, position, s, floor(dz) + c, True).start()
        move(k, position, n1, v, True).start()
        move(k, position, n2, v, True).start()
        move(k, position, s, other, True).start()

    def stage1(k):
        for dz in range(1, floors):
            owner = s * vocab + floor(dz) + c
            arrived(k, owner)
            move(k, owner, n1, v).start()
            move(k, owner, n2, v).start()
            move(k, owner, s, other).start()

    def stage2(k):
        for dz in range(floors):
            owner = n1 * vocab + floor(dz) + c
            arrived(k, owner)
            move(k, owner, n2, v).start()
            move(k, owner, s, other).start()

    def stage3(k):
        for source in (n2, far):
            for dz in range(floors):
                owner = source * vocab + floor(dz) + c
                arrived(k, owner)
                move(k, owner, s, other).start()

    def stage4(k):
        own_copy(k).wait()
        for section in range(sections):
            for level in range(floors):
                arrived(k, section * vocab + level * CORES + 1 - c)

    stages = (stage0, stage1, stage2, stage3, stage4)

    def run(plan):
        for index, k in plan:
            if k < CHUNKS:
                stages[index](k)

    for k in range(CHUNKS):
        head_copy(k).start()

    barrier = pltpu.get_barrier_semaphore()
    peers = [((s + d) % sections, v) for d in range(1, sections)]
    peers += [(s, (v + d) % vocab) for d in range(1, vocab)]
    for to_s, to_v in peers:
        pl.semaphore_signal(
            barrier, inc=1, device_id={"section": to_s, "vocab": to_v}, device_id_type=MESH
        )
    run_max[...] = jnp.full(run_max.shape, LOWEST, jnp.float32)
    run_sum[...] = jnp.zeros(run_sum.shape, jnp.float32)
    run_label[...] = jnp.zeros(run_label.shape, jnp.float32)
    target_ref[...] = (
        labels_ref[...] - position * vocab_rows - lax.broadcasted_iota(jnp.int32, (8, all_rows), 0)
    )
    pl.semaphore_wait(barrier, len(peers))

    run(((0, 0), (1, 0), (0, 1), (2, 0), (1, 1), (3, 0), (0, 2), (2, 1), (4, 0)))

    def product(k, i):
        return lax.dot_general(
            headv[k, pl.ds(i * TILE, TILE), :],
            hid[k],
            (((1,), (1,)), ((), ())),
            preferred_element_type=jnp.float32,
        )

    def soften(i):
        x = acc[pl.ds(i * TILE, TILE), :].reshape(TILE // 8, 8, all_rows)
        old = run_max[...]
        new = jnp.maximum(old, jnp.max(x, axis=0))
        run_max[...] = new
        run_sum[...] = run_sum[...] * jnp.exp(old - new) + jnp.sum(jnp.exp(x - new[None]), axis=0)
        place = 8 * lax.broadcasted_iota(jnp.int32, x.shape, 0) + i * TILE
        run_label[...] += jnp.sum(jnp.where(place == target_ref[...][None], x, 0.0), axis=0)

    tiles = vocab_rows // TILE
    for k in range(CHUNKS):
        head_copy(k).wait()
        plans = (((3, k + 1), (0, k + 3)), ((1, k + 2),), ((2, k + 2),), ())
        for part in range(SEGMENTS):
            run(plans[part])
            first = part * tiles // SEGMENTS
            last = (part + 1) * tiles // SEGMENTS

            def step(i, carry, k=k):
                here = pl.ds(i * TILE, TILE)
                if k == CHUNKS - 1:

                    @pl.when(i > 0)
                    def _():
                        soften(i - 1)

                if k == 0:
                    acc[here, :] = product(k, i)
                else:
                    acc[here, :] += product(k, i)
                return carry

            if k == CHUNKS - 1:
                if part == 0:

                    def whole(i, carry):
                        here = pl.ds(i * TILE, TILE)
                        soften(i - 1)
                        acc[here, :] += product(CHUNKS - 1, i)
                        return carry

                    acc[pl.ds(0, TILE), :] += product(k, 0)
                    lax.fori_loop(1, tiles, whole, 0)
            else:
                lax.fori_loop(first, last, step, 0)
        run(((4, k + 1),))
    soften(tiles - 1)

    top = jnp.max(run_max[...], axis=0, keepdims=True)
    total = jnp.sum(run_sum[...] * jnp.exp(run_max[...] - top), axis=0, keepdims=True)
    spread = top + jnp.log(total)
    label = jnp.sum(run_label[...], axis=0, keepdims=True)
    lines = all_rows // LANES
    for j in range(lines):
        stat_a[s, pl.ds(j, 1), :] = spread[:, j * LANES : (j + 1) * LANES]
        stat_a[s, pl.ds(lines + j, 1), :] = label[:, j * LANES : (j + 1) * LANES]

    def merge(buffer, count):
        values = [buffer[d] for d in range(count)]
        high = functools.reduce(jnp.maximum, [x[:lines] for x in values])
        weight = sum(jnp.exp(x[:lines] - high) for x in values)
        return high + jnp.log(weight), sum(x[lines:] for x in values)

    def share(buffer, mine, index, recv, to_s, to_v, slot):
        return pltpu.make_async_remote_copy(
            src_ref=buffer.at[mine],
            dst_ref=buffer.at[slot],
            send_sem=stat_send.at[index],
            recv_sem=recv.at[slot],
            device_id={"section": to_s, "vocab": to_v},
            device_id_type=MESH,
        )

    sent = []
    for d in range(1, sections):
        copy = share(stat_a, s, d - 1, recv_a, (s + d) % sections, v, s)
        copy.start()
        sent.append(copy)
    for d in range(1, sections):
        share(stat_a, s, d - 1, recv_a, (s + d) % sections, v, (s + d) % sections).wait_recv()
    spread, label = merge(stat_a, sections)
    stat_b[v, pl.ds(0, lines), :] = spread
    stat_b[v, pl.ds(lines, lines), :] = label
    for d in range(1, vocab):
        copy = share(stat_b, v, sections + d - 2, recv_b, s, (v + d) % vocab, v)
        copy.start()
        sent.append(copy)
    for d in range(1, vocab):
        share(stat_b, v, sections + d - 2, recv_b, s, (v + d) % vocab, (v + d) % vocab).wait_recv()
    spread, label = merge(stat_b, vocab)
    logprob = label - spread
    lp_ref[...] = logprob

    per_line = LANES // rows
    own = lp_ref[pl.ds(position // per_line, 1), :]
    own = pltpu.roll(own, (LANES - (position % per_line) * rows) % LANES, 1)
    token_ref[...] = own[:, :rows]

    per_seq = lines // SEQ_DP
    lane = lax.broadcasted_iota(jnp.int32, (1, LANES), 1)
    policy = jnp.zeros((1, LANES), jnp.float32)
    for q in range(SEQ_DP):
        sums = jnp.zeros((1, LANES), jnp.float32)
        counts = jnp.zeros((1, LANES), jnp.float32)
        for j in range(q * per_seq, (q + 1) * per_seq):
            weight = mask_ref[:, j * LANES : (j + 1) * LANES].astype(jnp.float32)
            sums += logprob[j : j + 1] * weight
            counts += weight
        mean = jnp.sum(sums, axis=1, keepdims=True) / jnp.sum(counts, axis=1, keepdims=True)
        policy += jnp.where(lane == pair_ref[0, q], mean, 0.0)
    policy_ref[...] = policy
    margin = jnp.zeros((1, LANES), jnp.float32)
    loss = jnp.zeros((1, LANES), jnp.float32)
    if solo:
        slots = ref_ref.shape[0]
        refs = jnp.zeros((1, LANES), jnp.float32)
        for q in range(slots):
            refs = jnp.where(lane == q, ref_ref[q], refs)
        gain = policy - refs
        for p in range(slots // 2):
            chosen = jnp.sum(jnp.where(lane == 2 * p, gain, 0.0), axis=1, keepdims=True)
            rejected = jnp.sum(jnp.where(lane == 2 * p + 1, gain, 0.0), axis=1, keepdims=True)
            margin = jnp.where(lane == p, beta_scale * (chosen - rejected), margin)
        soft = jnp.maximum(-margin, 0.0) + jnp.log1p(jnp.exp(-jnp.abs(margin)))
        soft = jnp.where(lane < slots // 2, soft, 0.0)
        loss = jnp.broadcast_to(jnp.sum(soft, axis=1, keepdims=True) / (slots // 2), (1, LANES))
    margin_ref[...] = margin
    loss_ref[...] = loss

    for copy in sent:
        copy.wait_send()
    for k in range(CHUNKS):
        span = hid.at[k, pl.ds(0, all_rows - rows)]
        pltpu.make_async_copy(span, span, send_sem.at[k]).wait()


def body(sections, vocab, replicas, hidden, head, labels, response_mask, seq_pair, ref_logp):
    rows, width = hidden.shape[1:]
    vocab_rows = head.shape[0]
    count = sections * vocab
    all_rows = rows * count
    lines = all_rows // LANES
    f32 = jnp.float32
    vmem = pl.BlockSpec(memory_space=pltpu.VMEM)
    smem = pl.BlockSpec(memory_space=pltpu.SMEM)
    anywhere = pl.BlockSpec(memory_space=pl.ANY)
    solo = replicas == 1
    token, policy, margin, loss = pl.pallas_call(
        functools.partial(kernel, sections, vocab, solo),
        out_shape=(
            jax.ShapeDtypeStruct((1, rows), f32),
            jax.ShapeDtypeStruct((1, LANES), f32),
            jax.ShapeDtypeStruct((1, LANES), f32),
            jax.ShapeDtypeStruct((1, LANES), f32),
        ),
        in_specs=[anywhere, anywhere, vmem, vmem, smem, smem],
        out_specs=(vmem, vmem, vmem, vmem),
        scratch_shapes=[
            pltpu.VMEM((CHUNKS, all_rows, width // CHUNKS), jnp.bfloat16),
            pltpu.VMEM((CHUNKS, vocab_rows, width // CHUNKS), jnp.bfloat16),
            pltpu.VMEM((vocab_rows, all_rows), f32),
            pltpu.VMEM((8, all_rows), f32),
            pltpu.VMEM((8, all_rows), f32),
            pltpu.VMEM((8, all_rows), f32),
            pltpu.VMEM((8, all_rows), jnp.int32),
            pltpu.VMEM((sections, 2 * lines, LANES), f32),
            pltpu.VMEM((vocab, 2 * lines, LANES), f32),
            pltpu.VMEM((lines, LANES), f32),
            pltpu.SemaphoreType.DMA((CHUNKS,)),
            pltpu.SemaphoreType.DMA((CHUNKS, count)),
            pltpu.SemaphoreType.DMA((CHUNKS,)),
            pltpu.SemaphoreType.DMA((CHUNKS,)),
            pltpu.SemaphoreType.DMA((sections + vocab,)),
            pltpu.SemaphoreType.DMA((sections,)),
            pltpu.SemaphoreType.DMA((vocab,)),
        ],
        compiler_params=pltpu.CompilerParams(
            collective_id=0, has_side_effects=True, vmem_limit_bytes=60 * 1024 * 1024
        ),
    )(hidden, head, labels, response_mask, seq_pair, ref_logp)
    slots = ref_logp.shape[0]
    if solo:
        return token, margin[0, : slots // 2], loss[0, 0]
    policy = lax.psum(policy[0, :slots], "dp")
    pair_margin = beta_scale * (policy[0::2] - ref_logp[0::2] - (policy[1::2] - ref_logp[1::2]))
    return token, pair_margin, jnp.mean(jnp.logaddexp(0.0, -pair_margin))


def solution(mesh):
    placed = (
        P("dp", ("section", "vocab"), None),
        P(("section", "vocab"), None),
        P("dp", None),
        P("dp", None),
        P("dp", None),
        P(),
    )
    shape = mesh.shape
    return jax.shard_map(
        functools.partial(body, shape["section"], shape["vocab"], shape["dp"]),
        mesh=mesh,
        in_specs=placed,
        out_specs=(P("dp", ("section", "vocab")), P(), P()),
        check_vma=False,
    )
```

time: 188 us -> 63.3 us (0.34)
  blocking collectives: 98.7 us -> 0 us
  Pallas kernels: 0 us -> 58.5 us
  waiting for transfers between devices: 41.9 us -> 0 us
  matrix products: 21 us -> 0 us
  between operations: 15.8 us -> 2.38 us
  other arithmetic: 7.75 us -> 0 us
    pallas_call x0 -> x1, Pallas kernels: none -> 58.5 us  [body(): pl.pallas_call(functools.partial(kernel, sections, vocab, solo), out_shap...]
    all_gather x1 -> x0, waiting for transfers between devices: 41.9 us -> none  [body(): gathered = lax.all_gather(chip_rows, 'section', axis=1, tiled=True)]
    psum x1 -> x0, blocking collectives: 40.9 us -> none  [body(): lax.psum((local_sum * jnp.exp(local_max - whole_max), label_part), ('sect...]
    pmax x1 -> x0, blocking collectives: 39.2 us -> none  [body(): whole_max = lax.pmax(local_max, ('section', 'vocab'))]
    dot_general x1 -> x0, matrix products: 21 us -> none  [body(): lax.dot_general(gathered[0], head, (((1,), (1,)), ((), ())), preferred_el...]
    all_gather x1 -> x0, blocking collectives: 18.5 us -> none  [body(): chip_rows = lax.all_gather(hidden, 'vocab', axis=1, tiled=True)]
    reduce_sum x5 -> x0, other arithmetic: 6.37 us -> none  [the longest x1 4.93 us: body(): jnp.sum(jnp.where(column == target[:, None], logits, 0.0), axis=1)]
  transfers between devices with their start and end apart: 1 -> 0, of which waited for: 1 -> 0; matrix products, arithmetic and copies ran while one was open for 2% -> 0% of each run, Pallas kernels for 0% -> 0%
where the time goes in v1:
time: 63.3 us; the launch traced here: 63.1 us
  Pallas kernels  58.5 us (92%)
  between operations  2.38 us (4%)
  local copies, waits for them, and re-layouts  2.29 us (4%)
    pallas_call x1, Pallas kernels, body(): pl.pallas_call(functools.partial(kernel, sections, vocab, solo), out_shap...  58.5 us

profile of v1, /device:TPU:0, one launch (start us, length us, event | category | flops | bytes accessed | tf_op | source)
XLA Modules:
  0.0 63.1 jit_solution(10132753481456986995)
XLA Ops:
  0.6 58.5 %shard_map.85 = (f32[1,16]{1,0:T(1,128)}, f32[1,128]{1,0:T(1,128)}, f32[1,128]{1,0:T(1,128)}, f32[1,128]{1,0:T(1,128)}) custom-call(bf16[1,16,3072]{2,1,0:T(8,128)(2,1)} %hidden_ref.1, bf16[4096,3072]{1,0:T(8,128)(2,1)} %head_ref.1, s32[1,512]{1,0:T(1,128)} %labels_ref.1, s32[1,512]{1,0:T(1,128)} %mask_ref.1, s32[1,4]{1,0:T(1,128)} %pair_ref.1, f32[4]{0:T(128)} %ref_ref.1), custom_call_target="tpu_custom_call" | custom-call | tf_op jit(solution)/shard_map/pallas_call | solution.py:319
  59.1 1.2 %slice_bitcast_fusion = f32[2]{0:T(128)} fusion(f32[1,128]{1,0:T(1,128)} %get-tuple-element.7), kind=kLoop, calls=%fused_computation | loop fusion | bytes 16 | tf_op jit(solution)/shard_map/squeeze | solution.py:354
  60.3 1.1 %copy.11 = f32[1,16]{1,0:T(1,128)} copy(f32[1,16]{1,0:T(1,128)} %get-tuple-element.12) | data formatting | bytes 128

commit v2 on v1

--- a/solution.py
+++ b/solution.py
@@ -10,8 +10,8 @@
 SEQ_DP = 4
 CORES = 2
 LANES = 128
-CHUNKS = 4
-TILE = 512
+CHUNKS = 2
+TILE = 1024
 SEGMENTS = 4
 LOWEST = -3.0e38
 
@@ -29,10 +29,7 @@
     mask_ref,
     pair_ref,
     ref_ref,
-    token_ref,
-    policy_ref,
-    margin_ref,
-    loss_ref,
+    out_ref,
     hid,
     headv,
     acc,
@@ -78,11 +75,10 @@
             own_sem.at[k],
         )
 
-    def move(k, owner, to_s, to_v, own=False):
+    def move(k, owner, to_s, to_v):
         here = hid.at[k, pl.ds(owner * rows, rows)]
-        src = hidden_ref.at[0, :, pl.ds(k * chunk, chunk)] if own else here
         return pltpu.make_async_remote_copy(
-            src_ref=src,
+            src_ref=here,
             dst_ref=here,
             send_sem=send_sem.at[k],
             recv_sem=recv_sem.at[k, owner],
@@ -99,12 +95,11 @@
         return ((z + dz) % floors) * CORES
 
     def stage0(k):
-        own_copy(k).start()
         for dz in range(1, floors):
-            move(k, position, s, floor(dz) + c, True).start()
-        move(k, position, n1, v, True).start()
-        move(k, position, n2, v, True).start()
-        move(k, position, s, other, True).start()
+            move(k, position, s, floor(dz) + c).start()
+        move(k, position, n1, v).start()
+        move(k, position, n2, v).start()
+        move(k, position, s, other).start()
 
     def stage1(k):
         for dz in range(1, floors):
@@ -129,7 +124,6 @@
                 move(k, owner, s, other).start()
 
     def stage4(k):
-        own_copy(k).wait()
         for section in range(sections):
             for level in range(floors):
                 arrived(k, section * vocab + level * CORES + 1 - c)
@@ -142,7 +136,7 @@
                 stages[index](k)
 
     for k in range(CHUNKS):
-        head_copy(k).start()
+        own_copy(k).start()
 
     barrier = pltpu.get_barrier_semaphore()
     peers = [((s + d) % sections, v) for d in range(1, sections)]
@@ -157,9 +151,13 @@
     target_ref[...] = (
         labels_ref[...] - position * vocab_rows - lax.broadcasted_iota(jnp.int32, (8, all_rows), 0)
     )
+    for k in range(CHUNKS):
+        own_copy(k).wait()
+    for k in range(CHUNKS):
+        head_copy(k).start()
     pl.semaphore_wait(barrier, len(peers))
 
-    run(((0, 0), (1, 0), (0, 1), (2, 0), (1, 1), (3, 0), (0, 2), (2, 1), (4, 0)))
+    run(((0, 0), (1, 0), (0, 1), (2, 0), (1, 1), (3, 0), (4, 0)))
 
     def product(k, i):
         return lax.dot_general(
@@ -181,7 +179,7 @@
     tiles = vocab_rows // TILE
     for k in range(CHUNKS):
         head_copy(k).wait()
-        plans = (((3, k + 1), (0, k + 3)), ((1, k + 2),), ((2, k + 2),), ())
+        plans = (((2, k + 1), (0, k + 2)), ((1, k + 2),), ((3, k + 1),), ())
         for part in range(SEGMENTS):
             run(plans[part])
             first = part * tiles // SEGMENTS
@@ -265,7 +263,8 @@
     per_line = LANES // rows
     own = lp_ref[pl.ds(position // per_line, 1), :]
     own = pltpu.roll(own, (LANES - (position % per_line) * rows) % LANES, 1)
-    token_ref[...] = own[:, :rows]
+    out_ref[...] = jnp.zeros(out_ref.shape, jnp.float32)
+    out_ref[0:1, :] = own
 
     per_seq = lines // SEQ_DP
     lane = lax.broadcasted_iota(jnp.int32, (1, LANES), 1)
@@ -279,7 +278,6 @@
             counts += weight
         mean = jnp.sum(sums, axis=1, keepdims=True) / jnp.sum(counts, axis=1, keepdims=True)
         policy += jnp.where(lane == pair_ref[0, q], mean, 0.0)
-    policy_ref[...] = policy
     margin = jnp.zeros((1, LANES), jnp.float32)
     loss = jnp.zeros((1, LANES), jnp.float32)
     if solo:
@@ -295,8 +293,9 @@
         soft = jnp.maximum(-margin, 0.0) + jnp.log1p(jnp.exp(-jnp.abs(margin)))
         soft = jnp.where(lane < slots // 2, soft, 0.0)
         loss = jnp.broadcast_to(jnp.sum(soft, axis=1, keepdims=True) / (slots // 2), (1, LANES))
-    margin_ref[...] = margin
-    loss_ref[...] = loss
+    out_ref[1:2, :] = margin
+    out_ref[2:3, :] = loss
+    out_ref[3:4, :] = policy
 
     for copy in sent:
         copy.wait_send()
@@ -316,16 +315,11 @@
     smem = pl.BlockSpec(memory_space=pltpu.SMEM)
     anywhere = pl.BlockSpec(memory_space=pl.ANY)
     solo = replicas == 1
-    token, policy, margin, loss = pl.pallas_call(
+    packed = pl.pallas_call(
         functools.partial(kernel, sections, vocab, solo),
-        out_shape=(
-            jax.ShapeDtypeStruct((1, rows), f32),
-            jax.ShapeDtypeStruct((1, LANES), f32),
-            jax.ShapeDtypeStruct((1, LANES), f32),
-            jax.ShapeDtypeStruct((1, LANES), f32),
-        ),
+        out_shape=jax.ShapeDtypeStruct((8, LANES), f32),
         in_specs=[anywhere, anywhere, vmem, vmem, smem, smem],
-        out_specs=(vmem, vmem, vmem, vmem),
+        out_specs=vmem,
         scratch_shapes=[
             pltpu.VMEM((CHUNKS, all_rows, width // CHUNKS), jnp.bfloat16),
             pltpu.VMEM((CHUNKS, vocab_rows, width // CHUNKS), jnp.bfloat16),
@@ -350,9 +344,10 @@
         ),
     )(hidden, head, labels, response_mask, seq_pair, ref_logp)
     slots = ref_logp.shape[0]
+    token = packed[:1, :rows]
     if solo:
-        return token, margin[0, : slots // 2], loss[0, 0]
-    policy = lax.psum(policy[0, :slots], "dp")
+        return token, packed[1, : slots // 2], packed[2, 0]
+    policy = lax.psum(packed[3, :slots], "dp")
     pair_margin = beta_scale * (policy[0::2] - ref_logp[0::2] - (policy[1::2] - ref_logp[1::2]))
     return token, pair_margin, jnp.mean(jnp.logaddexp(0.0, -pair_margin))
 

time: 63.3 us -> 51.3 us (0.81)
  Pallas kernels: 58.5 us -> 46.8 us
  between operations: 2.38 us -> 0.64 us
  local copies, waits for them, and re-layouts: 2.29 us -> 3.58 us
    pallas_call x1, Pallas kernels: 58.5 us -> 46.8 us  [body(): pl.pallas_call(functools.partial(kernel, sections, vocab, solo), out_shap...]
    slice x0 -> x2, local copies, waits for them, and re-layouts: none -> 2.39 us  [the longest x1 1.2 us: body(): return (token, packed[1, :slots // 2], packed[2, 0])]
    unnamed x1 -> x0, local copies, waits for them, and re-layouts: 1.11 us -> none
where the time goes in v2:
time: 51.3 us; the launch traced here: 51.1 us
  Pallas kernels  46.8 us (91%)
  local copies, waits for them, and re-layouts  3.58 us (7%)
  between operations  0.64 us (1%)
    pallas_call x1, Pallas kernels, body(): pl.pallas_call(functools.partial(kernel, sections, vocab, solo), out_shap...  46.8 us
    slice x1, local copies, waits for them, and re-layouts, body(): return (token, packed[1, :slots // 2], packed[2, 0])  1.2 us
    squeeze x1, local copies, waits for them, and re-layouts, body(): return (token, packed[1, :slots // 2], packed[2, 0])  1.19 us
    slice x1, local copies, waits for them, and re-layouts, body(): token = packed[:1, :rows]  1.19 us

profile of v2, /device:TPU:0, one launch (start us, length us, event | category | flops | bytes accessed | tf_op | source)
XLA Modules:
  0.0 51.1 jit_solution(15310967411568897594)
XLA Ops:
  0.6 46.8 %shard_map.85 = f32[8,128]{1,0:T(8,128)} custom-call(bf16[1,16,3072]{2,1,0:T(8,128)(2,1)} %hidden_ref.1, bf16[4096,3072]{1,0:T(8,128)(2,1)} %head_ref.1, s32[1,512]{1,0:T(1,128)} %labels_ref.1, s32[1,512]{1,0:T(1,128)} %mask_ref.1, s32[1,4]{1,0:T(1,128)} %pair_ref.1, f32[4]{0:T(128)} %ref_ref.1), custom_call_target="tpu_custom_call" | custom-call | tf_op jit(solution)/shard_map/pallas_call | solution.py:318
  47.5 1.2 %slice.11 = f32[1,1]{1,0:T(1,128)} slice(f32[8,128]{1,0:T(8,128)} %shard_map.85), slice={[2:3], [0:1]} | slice | bytes 8 | tf_op jit(solution)/shard_map/slice | solution.py:349
  48.7 1.2 %slice_bitcast_fusion = f32[2]{0:T(128)} fusion(f32[8,128]{1,0:T(8,128)} %shard_map.85), kind=kLoop, calls=%fused_computation | loop fusion | bytes 16 | tf_op jit(solution)/shard_map/squeeze | solution.py:349
  49.9 1.2 %slice.9 = f32[1,16]{1,0:T(1,128)} slice(f32[8,128]{1,0:T(8,128)} %shard_map.85), slice={[0:1], [0:16]} | slice | bytes 128 | tf_op jit(solution)/shard_map/slice | solution.py:347
